TPU v7x, 128 devices: a whole 4x4x4 slice. The times are simulated.
128 devices in a mesh: dp: 32 (over z, y, core), tm: 4 (over x).
Axes of the slice: x: 4, y: 4, z: 4, core: 2. Of those that a mesh axis runs over, the one named last changes fastest.
Arguments:
- student: bfloat16 [256, 1024, 128], P(('dp', 'tm')), may hold values from -6 to 6
- teacher: bfloat16 [256, 1024, 128], P(('dp', 'tm')), may hold values from -200 to 200
- partner_dp: int32 [256, 8], replicated, may hold values from 0 to 31, all different within a row; in each aligned block of 2 rows (0 to 1, 2 to 3, ...) no two rows name the same one
- partner_slot: int32 [256, 8], replicated, may hold values from 0 to 1
- valid_frames: int32 [256], replicated, may hold values from 256 to 1024, as said below
Outputs:
- loss: float32 [], replicated
- grad_student: bfloat16 [256, 1024, 128], P(('dp', 'tm'))
Inputs may be any that keep to these rules, and one draw needn't show every extreme that they name: `partner_dp`: among the partner entries of the 2 blocks of one device no dp index appears more than 1 times; the 8 entries of one block are distinct. A partner may be the block itself. `valid_frames`: block 0 is full and block 1 has the fewest valid frames.
All inputs are finite; a program needn't handle non-finite values.
Results may differ from a plain program's by a relative error of at most 0.0042.
Values may be sent and summed in bfloat16 or wider, within the bound.
A program may use at most 64 MiB of HBM per device.

v0:
```python
import math
import jax
import jax.numpy as jnp
from jax import lax
from jax.sharding import PartitionSpec as P

NEG_FILL = -1e30


def body(student, teacher, partner_dp, partner_slot, valid_frames):
    peer_count = lax.axis_size("dp")
    time_count = lax.axis_size("tm")
    my_dp = lax.axis_index("dp")
    my_tm = lax.axis_index("tm")
    local_blocks, frames, proj_width = student.shape
    partner_count = partner_dp.shape[1]
    entries = local_blocks * partner_count
    slot_depth = (entries + peer_count - 1) // peer_count
    slot_total = peer_count * slot_depth
    score_scale = 1.0 / math.sqrt(proj_width)
    dest_all = lax.dynamic_index_in_dim(
        partner_dp.reshape(peer_count, time_count, entries), my_tm, 1, keepdims=False
    )
    source_all = lax.dynamic_index_in_dim(
        partner_slot.reshape(peer_count, time_count, entries), my_tm, 1, keepdims=False
    )
    earlier = jnp.tril(jnp.ones((entries, entries), jnp.int32), -1)
    same_dest = (dest_all[:, :, None] == dest_all[:, None, :]).astype(jnp.int32)
    rank_all = jnp.sum(same_dest * earlier[None], axis=2)
    my_dest = lax.dynamic_index_in_dim(dest_all, my_dp, 0, keepdims=False)
    my_source = lax.dynamic_index_in_dim(source_all, my_dp, 0, keepdims=False)
    my_rank = lax.dynamic_index_in_dim(rank_all, my_dp, 0, keepdims=False)
    entry_slot = my_dest * slot_depth + my_rank
    depth_ids = jnp.arange(slot_depth, dtype=jnp.int32)
    wanted = (dest_all == my_dp)[:, :, None] & (rank_all[:, :, None] == depth_ids[None, None, :])
    in_use = jnp.any(wanted, axis=1).reshape(slot_total)
    local_block = jnp.sum(jnp.where(wanted, source_all[:, :, None], 0), axis=1).reshape(slot_total)
    block_base = (my_dp * time_count + my_tm) * local_blocks
    frame_ids = jnp.arange(frames, dtype=jnp.int32)
    own_len = lax.dynamic_slice_in_dim(valid_frames, block_base, local_blocks)
    far_len = valid_frames[(my_dest * time_count + my_tm) * local_blocks + my_source]
    query_ok = frame_ids[None, :] < own_len[:, None]
    everyone = lax.all_gather(teacher, "dp", axis=0, tiled=True)
    far_keys = everyone[my_dest * local_blocks + my_source]
    keys_all = jnp.concatenate(
        [teacher[:, None], far_keys.reshape(local_blocks, partner_count, frames, proj_width)],
        axis=1,
    )
    lens_all = jnp.concatenate(
        [own_len[:, None], far_len.reshape(local_blocks, partner_count)], axis=1
    )
    keys_tiled = jnp.swapaxes(keys_all, 0, 1)
    lens_tiled = jnp.swapaxes(lens_all, 0, 1)

    def first_pass(inputs):
        key_block, lengths = inputs
        scores = (
            jnp.einsum("aie,aje->aij", student, key_block, preferred_element_type=jnp.float32)
            * score_scale
        )
        key_ok = frame_ids[None, :] < lengths[:, None]
        row_masked = jnp.where(key_ok[:, None, :], scores, NEG_FILL)
        row_best = jnp.max(row_masked, axis=2)
        row_sum = jnp.sum(jnp.exp(row_masked - row_best[:, :, None]), axis=2)
        col_masked = jnp.where(query_ok[:, :, None], scores, NEG_FILL)
        col_best = jnp.max(col_masked, axis=1)
        col_sum = jnp.sum(jnp.exp(col_masked - col_best[:, None, :]), axis=1)
        return (row_best, row_sum, col_best, col_sum)

    row_best, row_sum, col_best, col_sum = lax.map(first_pass, (keys_tiled, lens_tiled))
    row_top = jnp.max(row_best, axis=0)
    row_lse = row_top + jnp.log(jnp.sum(row_sum * jnp.exp(row_best - row_top[None]), axis=0))
    far_best = jnp.swapaxes(col_best[1:], 0, 1).reshape(entries, frames)
    far_sum = jnp.swapaxes(col_sum[1:], 0, 1).reshape(entries, frames)
    back_best = jnp.full((slot_total, frames), NEG_FILL, jnp.float32).at[entry_slot].set(far_best)
    back_sum = jnp.zeros((slot_total, frames), jnp.float32).at[entry_slot].set(far_sum)
    inc_best, inc_sum = (
        lax.all_to_all(back_best, "dp", split_axis=0, concat_axis=0, tiled=True),
        lax.all_to_all(back_sum, "dp", split_axis=0, concat_axis=0, tiled=True),
    )
    chosen = (local_block[:, None] == jnp.arange(local_blocks, dtype=jnp.int32)[None, :]) & in_use[
        :, None
    ]
    cand_best = jnp.where(chosen[:, :, None], inc_best[:, None, :], NEG_FILL)
    merged_best = jnp.maximum(col_best[0], jnp.max(cand_best, axis=0))
    merged_sum = col_sum[0] * jnp.exp(col_best[0] - merged_best)
    merged_sum = merged_sum + jnp.sum(
        jnp.where(
            chosen[:, :, None], inc_sum[:, None, :] * jnp.exp(cand_best - merged_best[None]), 0.0
        ),
        axis=0,
    )
    col_lse = merged_best + jnp.log(jnp.where(query_ok, merged_sum, 1.0))
    lse_out = jnp.where(in_use[:, None], col_lse[local_block], 0.0)
    lse_in = lax.all_to_all(lse_out, "dp", split_axis=0, concat_axis=0, tiled=True)
    far_lse = lse_in[entry_slot].reshape(local_blocks, partner_count, frames)
    lse_tiled = jnp.swapaxes(jnp.concatenate([col_lse[:, None], far_lse], axis=1), 0, 1)
    positive = (
        jnp.sum(student.astype(jnp.float32) * teacher.astype(jnp.float32), axis=2) * score_scale
    )
    row_terms = jnp.sum(jnp.where(query_ok, row_lse - positive, 0.0))
    col_terms = jnp.sum(jnp.where(query_ok, col_lse - positive, 0.0))
    loss_sum = lax.psum(0.5 * (row_terms + col_terms), ("dp", "tm"))
    loss = loss_sum / jnp.sum(valid_frames).astype(jnp.float32)
    diagonal = frame_ids[:, None] == frame_ids[None, :]

    def second_pass(inputs):
        key_block, lengths, key_lse, tile_index = inputs
        scores = (
            jnp.einsum("aie,aje->aij", student, key_block, preferred_element_type=jnp.float32)
            * score_scale
        )
        key_ok = frame_ids[None, :] < lengths[:, None]
        pair_ok = query_ok[:, :, None] & key_ok[:, None, :]
        prob_row = jnp.exp(scores - row_lse[:, :, None])
        prob_col = jnp.exp(scores - key_lse[:, None, :])
        grad_scores = jnp.where(pair_ok, 0.5 * (prob_row + prob_col), 0.0)
        grad_scores = grad_scores - jnp.where(
            (tile_index == 0) & diagonal[None] & query_ok[:, :, None], 1.0, 0.0
        )
        return jnp.einsum(
            "aij,aje->aie",
            grad_scores.astype(jnp.bfloat16),
            key_block,
            preferred_element_type=jnp.float32,
        )

    tile_ids = jnp.arange(partner_count + 1, dtype=jnp.int32)
    pieces = lax.map(second_pass, (keys_tiled, lens_tiled, lse_tiled, tile_ids))
    grad_student = (jnp.sum(pieces, axis=0) * score_scale).astype(jnp.bfloat16)
    return (loss, grad_student)


def solution(mesh):
    placed = (P(("dp", "tm"), None, None), P(("dp", "tm"), None, None), P(), P(), P())
    return jax.shard_map(
        body,
        mesh=mesh,
        in_specs=placed,
        out_specs=(P(), P(("dp", "tm"), None, None)),
        check_vma=False,
    )
```

profile of v0, /device:TPU:1, one launch (start us, length us, event | category | flops | bytes accessed | tf_op | source)
XLA Modules:
  0.0 386.1 jit_solution(9657005875069770102)
XLA Ops:
  8.0 0.8 dynamic_slice.42
  9.6 0.8 copy.92
  10.5 0.8 copy.93
  12.1 1.3 gather_fusion
  13.7 1.6 multiply_reduce_fusion
  15.3 71.3 %all-gather.2.cloned.1.call-done = bf16[64,1024,128]{2,1,0:T(8,128)(2,1)} async-done(((bf16[2,1024,128]{2,1,0:T(8,128)(2,1)}), bf16[64,1024,128]{2,1,0:T(8,128)(2,1)}) %all-gather.2.cloned.1.call-update) | async-done | bytes 16777232 | tf_op jit(solution)/shard_map/all_gather | solution.py:43
  86.6 8.8 %gather_fusion.1 = bf16[16,1024,128]{2,1,0:T(8,128)(2,1)} fusion(bf16[64,1024,128]{2,1,0:T(8,128)(2,1)} %all-gather.2.cloned.1.call-done, s32[1024]{0:T(1024)S(1)} %pad_clamp_fusion.2), kind=kCustom, calls=%fused_computation.1 | custom fusion | bytes 8388672 | tf_op jit(solution)/shard_map/gather | solution.py:44
  95.3 2.7 maximum_bitcast_fusion
  98.0 2.7 copy.96
  100.7 74.8 %while.28 = (s32[]{:T(128)}, f32[9,2,1024]{2,1,0:T(2,128)S(1)}, f32[9,2,1024]{2,1,0:T(2,128)S(1)}, f32[9,2,1024]{2,1,0:T(2,128)S(1)}, f32[9,2,1024]{2,1,0:T(2,12...) while((s32[]{:T(128)}, f32[9,2,1024]{2,1,0:T(2,128)S(1)}, ...), condition=%wide.region_5.6_spmd.clone, body=%wide.region_0.5_spmd.clone.sunk | while | flops 562032640 | bytes 17952924 | solution.py:70
  100.8 3.5 bitcast_reduce_fusion.3
  104.3 4.6 %fusion.84 = (f32[2,1024]{1,0:T(2,128)S(1)}, f32[2,1024]{1,0:T(2,128)S(1)}) fusion(f32[2,1024,1024]{2,1,0:T(8,128)S(1)} %get-tuple-element.479, f32[2,1024]{1,0:T(2,128)S(1)} %get-tuple-element.480, pred[2,1024]{1,0:T(4,128)(4,1)S(1)} %iota_compare_fusion.10, f32[2,1024]{1,0:T(2,128)S(1)} %get-tuple-element.481, ...), kind=kLoop, calls=%fused_computation.14.clone.1 | loop fusion | flops 14675968 | bytes 8425472 | tf_op jit(solution)/shard_map/while/body/eval_jaxpr/reduce_sum | solution.py:67
  109.1 3.5 bitcast_reduce_fusion.3
  112.6 4.6 %fusion.84 = (f32[2,1024]{1,0:T(2,128)S(1)}, f32[2,1024]{1,0:T(2,128)S(1)}) fusion(f32[2,1024,1024]{2,1,0:T(8,128)S(1)} %get-tuple-element.479, f32[2,1024]{1,0:T(2,128)S(1)} %get-tuple-element.480, pred[2,1024]{1,0:T(4,128)(4,1)S(1)} %iota_compare_fusion.10, f32[2,1024]{1,0:T(2,128)S(1)} %get-tuple-element.481, ...), kind=kLoop, calls=%fused_computation.14.clone.1 | loop fusion | flops 14675968 | bytes 8425472 | tf_op jit(solution)/shard_map/while/body/eval_jaxpr/reduce_sum | solution.py:67
  117.5 3.5 bitcast_reduce_fusion.3
  120.9 4.6 %fusion.84 = (f32[2,1024]{1,0:T(2,128)S(1)}, f32[2,1024]{1,0:T(2,128)S(1)}) fusion(f32[2,1024,1024]{2,1,0:T(8,128)S(1)} %get-tuple-element.479, f32[2,1024]{1,0:T(2,128)S(1)} %get-tuple-element.480, pred[2,1024]{1,0:T(4,128)(4,1)S(1)} %iota_compare_fusion.10, f32[2,1024]{1,0:T(2,128)S(1)} %get-tuple-element.481, ...), kind=kLoop, calls=%fused_computation.14.clone.1 | loop fusion | flops 14675968 | bytes 8425472 | tf_op jit(solution)/shard_map/while/body/eval_jaxpr/reduce_sum | solution.py:67
  125.8 3.5 bitcast_reduce_fusion.3
  129.2 4.6 %fusion.84 = (f32[2,1024]{1,0:T(2,128)S(1)}, f32[2,1024]{1,0:T(2,128)S(1)}) fusion(f32[2,1024,1024]{2,1,0:T(8,128)S(1)} %get-tuple-element.479, f32[2,1024]{1,0:T(2,128)S(1)} %get-tuple-element.480, pred[2,1024]{1,0:T(4,128)(4,1)S(1)} %iota_compare_fusion.10, f32[2,1024]{1,0:T(2,128)S(1)} %get-tuple-element.481, ...), kind=kLoop, calls=%fused_computation.14.clone.1 | loop fusion | flops 14675968 | bytes 8425472 | tf_op jit(solution)/shard_map/while/body/eval_jaxpr/reduce_sum | solution.py:67
  134.1 3.5 bitcast_reduce_fusion.3
  137.6 4.6 %fusion.84 = (f32[2,1024]{1,0:T(2,128)S(1)}, f32[2,1024]{1,0:T(2,128)S(1)}) fusion(f32[2,1024,1024]{2,1,0:T(8,128)S(1)} %get-tuple-element.479, f32[2,1024]{1,0:T(2,128)S(1)} %get-tuple-element.480, pred[2,1024]{1,0:T(4,128)(4,1)S(1)} %iota_compare_fusion.10, f32[2,1024]{1,0:T(2,128)S(1)} %get-tuple-element.481, ...), kind=kLoop, calls=%fused_computation.14.clone.1 | loop fusion | flops 14675968 | bytes 8425472 | tf_op jit(solution)/shard_map/while/body/eval_jaxpr/reduce_sum | solution.py:67
  142.4 3.5 bitcast_reduce_fusion.3
  145.9 4.6 %fusion.84 = (f32[2,1024]{1,0:T(2,128)S(1)}, f32[2,1024]{1,0:T(2,128)S(1)}) fusion(f32[2,1024,1024]{2,1,0:T(8,128)S(1)} %get-tuple-element.479, f32[2,1024]{1,0:T(2,128)S(1)} %get-tuple-element.480, pred[2,1024]{1,0:T(4,128)(4,1)S(1)} %iota_compare_fusion.10, f32[2,1024]{1,0:T(2,128)S(1)} %get-tuple-element.481, ...), kind=kLoop, calls=%fused_computation.14.clone.1 | loop fusion | flops 14675968 | bytes 8425472 | tf_op jit(solution)/shard_map/while/body/eval_jaxpr/reduce_sum | solution.py:67
  150.7 3.5 bitcast_reduce_fusion.3
  154.2 4.6 %fusion.84 = (f32[2,1024]{1,0:T(2,128)S(1)}, f32[2,1024]{1,0:T(2,128)S(1)}) fusion(f32[2,1024,1024]{2,1,0:T(8,128)S(1)} %get-tuple-element.479, f32[2,1024]{1,0:T(2,128)S(1)} %get-tuple-element.480, pred[2,1024]{1,0:T(4,128)(4,1)S(1)} %iota_compare_fusion.10, f32[2,1024]{1,0:T(2,128)S(1)} %get-tuple-element.481, ...), kind=kLoop, calls=%fused_computation.14.clone.1 | loop fusion | flops 14675968 | bytes 8425472 | tf_op jit(solution)/shard_map/while/body/eval_jaxpr/reduce_sum | solution.py:67
  159.0 3.5 bitcast_reduce_fusion.3
  162.5 4.6 %fusion.84 = (f32[2,1024]{1,0:T(2,128)S(1)}, f32[2,1024]{1,0:T(2,128)S(1)}) fusion(f32[2,1024,1024]{2,1,0:T(8,128)S(1)} %get-tuple-element.479, f32[2,1024]{1,0:T(2,128)S(1)} %get-tuple-element.480, pred[2,1024]{1,0:T(4,128)(4,1)S(1)} %iota_compare_fusion.10, f32[2,1024]{1,0:T(2,128)S(1)} %get-tuple-element.481, ...), kind=kLoop, calls=%fused_computation.14.clone.1 | loop fusion | flops 14675968 | bytes 8425472 | tf_op jit(solution)/shard_map/while/body/eval_jaxpr/reduce_sum | solution.py:67
  167.3 3.5 bitcast_reduce_fusion.3
  170.8 4.6 %fusion.84 = (f32[2,1024]{1,0:T(2,128)S(1)}, f32[2,1024]{1,0:T(2,128)S(1)}) fusion(f32[2,1024,1024]{2,1,0:T(8,128)S(1)} %get-tuple-element.479, f32[2,1024]{1,0:T(2,128)S(1)} %get-tuple-element.480, pred[2,1024]{1,0:T(4,128)(4,1)S(1)} %iota_compare_fusion.10, f32[2,1024]{1,0:T(2,128)S(1)} %get-tuple-element.481, ...), kind=kLoop, calls=%fused_computation.14.clone.1 | loop fusion | flops 14675968 | bytes 8425472 | tf_op jit(solution)/shard_map/while/body/eval_jaxpr/reduce_sum | solution.py:67
  177.0 5.4 %all-to-all-start = ((f32[32,1,1024]{2,1,0:T(1,128)}), f32[32,1,1024]{2,1,0:T(1,128)S(1)}, u32[]{:S(2)}, u32[]{:S(2)}) async-start(f32[32,1,1024]{2,1,0:T(1,128)} %all_to_all.18), calls=%async_computation | async-start | bytes 262144 | tf_op jit(solution)/shard_map/all_to_all | solution.py:78
  184.7 5.3 %all-to-all-done = f32[32,1,1024]{2,1,0:T(1,128)S(1)} async-done(((f32[32,1,1024]{2,1,0:T(1,128)}), f32[32,1,1024]{2,1,0:T(1,128)S(1)}, u32[]{:S(2)}, u32[]{:S(2)}) %all-to-all-start) | async-done | bytes 131104 | tf_op jit(solution)/shard_map/all_to_all | solution.py:78
  190.0 3.9 %all-to-all-start.1 = ((f32[32,1,1024]{2,1,0:T(1,128)}), f32[32,1,1024]{2,1,0:T(1,128)S(1)}, u32[]{:S(2)}, u32[]{:S(2)}) async-start(f32[32,1,1024]{2,1,0:T(1,128)} %all_to_all.20), calls=%async_computation.1 | async-start | bytes 262144 | tf_op jit(solution)/shard_map/all_to_all | solution.py:79
  194.1 7.6 %all-to-all-done.1 = f32[32,1,1024]{2,1,0:T(1,128)S(1)} async-done(((f32[32,1,1024]{2,1,0:T(1,128)}), f32[32,1,1024]{2,1,0:T(1,128)S(1)}, u32[]{:S(2)}, u32[]{:S(2)}) %all-to-all-start.1) | async-done | bytes 131104 | tf_op jit(solution)/shard_map/all_to_all | solution.py:79
  204.4 64.1 %psum.7 = f32[]{:T(128)} all-reduce(f32[]{:T(128)S(6)} %mul.113), channel_id=1, replica_groups=mesh['dp'=32,'tm'=4] {'dp','tm'}, use_global_device_ids=true, to_apply=%region_18.19 | all-reduce | flops 1 | bytes 8 | tf_op jit(solution)/shard_map/psum | solution.py:103
  269.3 0.8 copy.101
  270.1 4.7 %all-to-all-start.2 = ((f32[32,1,1024]{2,1,0:T(1,128)}), f32[32,1,1024]{2,1,0:T(1,128)S(1)}, u32[]{:S(2)}, u32[]{:S(2)}) async-start(f32[32,1,1024]{2,1,0:T(1,128)} %copy.101), calls=%async_computation.2 | async-start | bytes 262144 | tf_op jit(solution)/shard_map/all_to_all | solution.py:95
  275.6 6.9 %all-to-all-done.2 = f32[32,1,1024]{2,1,0:T(1,128)S(1)} async-done(((f32[32,1,1024]{2,1,0:T(1,128)}), f32[32,1,1024]{2,1,0:T(1,128)S(1)}, u32[]{:S(2)}, u32[]{:S(2)}) %all-to-all-start.2) | async-done | bytes 131104 | tf_op jit(solution)/shard_map/all_to_all | solution.py:95
  283.1 89.9 %while.29 = (s32[]{:T(128)}, f32[9,2,1024,128]{3,2,1,0:T(8,128)}, s32[9,2]{1,0:T(8,128)S(1)}, bf16[9,2,1024,128]{3,2,1,0:T(8,128)(2,1)}, bf16[2,1024,128]{2,1,0:...) while((s32[]{:T(128)}, f32[9,2,1024,128]{3,2,1,0:T(8,128)}, ...), condition=%wide.region_21.22_spmd.clone, body=%wide.region_20.21_spmd.clone.sunk | while | flops 1098911744 | bytes 4761267 | solution.py:129
  284.8 8.3 %fusion.91 = f32[9,2,1024,128]{3,2,1,0:T(8,128)} fusion(f32[9,2,1024,128]{3,2,1,0:T(8,128)} %get-tuple-element.541, s32[]{:T(128)S(6)} %copy.138, f32[2,1024]{1,0:T(2,128)S(1)} %dynamic-slice_bitcast_fusion.3, f32[2,1024]{1,0:T(2,128)S(1)} %get-tuple-element.556, pred[1024,1024]{0,1:T(8,128)(4,1)S(1)} %fusion.89, ...), kind=kOutput, calls=%fused_computation.39.clone.1 | convolution fusion | flops 1096810496 | bytes 3692032 | tf_op jit(solution)/shard_map/while/body/eval_jaxpr/aij,aje->aie/dot_general | solution.py:121
  294.8 8.3 %fusion.91 = f32[9,2,1024,128]{3,2,1,0:T(8,128)} fusion(f32[9,2,1024,128]{3,2,1,0:T(8,128)} %get-tuple-element.541, s32[]{:T(128)S(6)} %copy.138, f32[2,1024]{1,0:T(2,128)S(1)} %dynamic-slice_bitcast_fusion.3, f32[2,1024]{1,0:T(2,128)S(1)} %get-tuple-element.556, pred[1024,1024]{0,1:T(8,128)(4,1)S(1)} %fusion.89, ...), kind=kOutput, calls=%fused_computation.39.clone.1 | convolution fusion | flops 1096810496 | bytes 3692032 | tf_op jit(solution)/shard_map/while/body/eval_jaxpr/aij,aje->aie/dot_general | solution.py:121
  304.8 8.3 %fusion.91 = f32[9,2,1024,128]{3,2,1,0:T(8,128)} fusion(f32[9,2,1024,128]{3,2,1,0:T(8,128)} %get-tuple-element.541, s32[]{:T(128)S(6)} %copy.138, f32[2,1024]{1,0:T(2,128)S(1)} %dynamic-slice_bitcast_fusion.3, f32[2,1024]{1,0:T(2,128)S(1)} %get-tuple-element.556, pred[1024,1024]{0,1:T(8,128)(4,1)S(1)} %fusion.89, ...), kind=kOutput, calls=%fused_computation.39.clone.1 | convolution fusion | flops 1096810496 | bytes 3692032 | tf_op jit(solution)/shard_map/while/body/eval_jaxpr/aij,aje->aie/dot_general | solution.py:121
  314.8 8.3 %fusion.91 = f32[9,2,1024,128]{3,2,1,0:T(8,128)} fusion(f32[9,2,1024,128]{3,2,1,0:T(8,128)} %get-tuple-element.541, s32[]{:T(128)S(6)} %copy.138, f32[2,1024]{1,0:T(2,128)S(1)} %dynamic-slice_bitcast_fusion.3, f32[2,1024]{1,0:T(2,128)S(1)} %get-tuple-element.556, pred[1024,1024]{0,1:T(8,128)(4,1)S(1)} %fusion.89, ...), kind=kOutput, calls=%fused_computation.39.clone.1 | convolution fusion | flops 1096810496 | bytes 3692032 | tf_op jit(solution)/shard_map/while/body/eval_jaxpr/aij,aje->aie/dot_general | solution.py:121
  324.7 8.3 %fusion.91 = f32[9,2,1024,128]{3,2,1,0:T(8,128)} fusion(f32[9,2,1024,128]{3,2,1,0:T(8,128)} %get-tuple-element.541, s32[]{:T(128)S(6)} %copy.138, f32[2,1024]{1,0:T(2,128)S(1)} %dynamic-slice_bitcast_fusion.3, f32[2,1024]{1,0:T(2,128)S(1)} %get-tuple-element.556, pred[1024,1024]{0,1:T(8,128)(4,1)S(1)} %fusion.89, ...), kind=kOutput, calls=%fused_computation.39.clone.1 | convolution fusion | flops 1096810496 | bytes 3692032 | tf_op jit(solution)/shard_map/while/body/eval_jaxpr/aij,aje->aie/dot_general | solution.py:121
  334.7 8.3 %fusion.91 = f32[9,2,1024,128]{3,2,1,0:T(8,128)} fusion(f32[9,2,1024,128]{3,2,1,0:T(8,128)} %get-tuple-element.541, s32[]{:T(128)S(6)} %copy.138, f32[2,1024]{1,0:T(2,128)S(1)} %dynamic-slice_bitcast_fusion.3, f32[2,1024]{1,0:T(2,128)S(1)} %get-tuple-element.556, pred[1024,1024]{0,1:T(8,128)(4,1)S(1)} %fusion.89, ...), kind=kOutput, calls=%fused_computation.39.clone.1 | convolution fusion | flops 1096810496 | bytes 3692032 | tf_op jit(solution)/shard_map/while/body/eval_jaxpr/aij,aje->aie/dot_general | solution.py:121
  344.7 8.3 %fusion.91 = f32[9,2,1024,128]{3,2,1,0:T(8,128)} fusion(f32[9,2,1024,128]{3,2,1,0:T(8,128)} %get-tuple-element.541, s32[]{:T(128)S(6)} %copy.138, f32[2,1024]{1,0:T(2,128)S(1)} %dynamic-slice_bitcast_fusion.3, f32[2,1024]{1,0:T(2,128)S(1)} %get-tuple-element.556, pred[1024,1024]{0,1:T(8,128)(4,1)S(1)} %fusion.89, ...), kind=kOutput, calls=%fused_computation.39.clone.1 | convolution fusion | flops 1096810496 | bytes 3692032 | tf_op jit(solution)/shard_map/while/body/eval_jaxpr/aij,aje->aie/dot_general | solution.py:121
  354.6 8.3 %fusion.91 = f32[9,2,1024,128]{3,2,1,0:T(8,128)} fusion(f32[9,2,1024,128]{3,2,1,0:T(8,128)} %get-tuple-element.541, s32[]{:T(128)S(6)} %copy.138, f32[2,1024]{1,0:T(2,128)S(1)} %dynamic-slice_bitcast_fusion.3, f32[2,1024]{1,0:T(2,128)S(1)} %get-tuple-element.556, pred[1024,1024]{0,1:T(8,128)(4,1)S(1)} %fusion.89, ...), kind=kOutput, calls=%fused_computation.39.clone.1 | convolution fusion | flops 1096810496 | bytes 3692032 | tf_op jit(solution)/shard_map/while/body/eval_jaxpr/aij,aje->aie/dot_general | solution.py:121
  364.6 8.4 %fusion.91 = f32[9,2,1024,128]{3,2,1,0:T(8,128)} fusion(f32[9,2,1024,128]{3,2,1,0:T(8,128)} %get-tuple-element.541, s32[]{:T(128)S(6)} %copy.138, f32[2,1024]{1,0:T(2,128)S(1)} %dynamic-slice_bitcast_fusion.3, f32[2,1024]{1,0:T(2,128)S(1)} %get-tuple-element.556, pred[1024,1024]{0,1:T(8,128)(4,1)S(1)} %fusion.89, ...), kind=kOutput, calls=%fused_computation.39.clone.1 | convolution fusion | flops 1096810496 | bytes 3692032 | tf_op jit(solution)/shard_map/while/body/eval_jaxpr/aij,aje->aie/dot_general | solution.py:121
  373.0 4.2 %reduce_sum.113 = f32[2,1024,128]{2,1,0:T(8,128)S(1)} reduce(f32[9,2,1024,128]{3,2,1,0:T(8,128)} %get-tuple-element.118, f32[]{:T(128)} %constant.134.clone.1), dimensions={0}, to_apply=%region_22.23 | reduce | flops 2097152 | bytes 10485764 | tf_op jit(solution)/shard_map/reduce_sum | solution.py:130
  377.3 0.9 multiply_convert_fusion
  (150 shorter events, 19.7 us)
Async XLA Ops:
  7.2 88.2 %copy-start.1 = (bf16[2,1024,128]{2,1,0:T(8,128)(2,1)S(1)}, bf16[2,1024,128]{2,1,0:T(8,128)(2,1)}, u32[]{:S(2)}) copy-start(bf16[2,1024,128]{2,1,0:T(8,128)(2,1)} %param.10) | copy-start | bytes 1572868
  7.2 79.4 %all-gather.2.cloned.1.call-start = ((), (), s32[]{:S(2)}) async-start(), calls=%async_computation.3 | async-start | bytes 17301504 | tf_op jit(solution)/shard_map/all_gather | solution.py:43
  95.3 5.3 %copy-start.2 = (bf16[2,1024,128]{2,1,0:T(8,128)(2,1)S(1)}, bf16[2,1024,128]{2,1,0:T(8,128)(2,1)}, u32[]{:S(2)}) copy-start(bf16[2,1024,128]{2,1,0:T(8,128)(2,1)} %param.9) | copy-start | bytes 1572868
  100.7 81.7 %copy-start = (s32[256]{0:T(256)S(1)}, s32[256]{0:T(256)}, u32[]{:S(2)}) copy-start(s32[256]{0:T(256)} %param.13) | copy-start | bytes 3076
  177.0 13.0 %all-to-all-start = ((f32[32,1,1024]{2,1,0:T(1,128)}), f32[32,1,1024]{2,1,0:T(1,128)S(1)}, u32[]{:S(2)}, u32[]{:S(2)}) async-start(f32[32,1,1024]{2,1,0:T(1,128)} %all_to_all.18), calls=%async_computation | async-start | bytes 262144 | tf_op jit(solution)/shard_map/all_to_all | solution.py:78
  190.0 11.6 %all-to-all-start.1 = ((f32[32,1,1024]{2,1,0:T(1,128)}), f32[32,1,1024]{2,1,0:T(1,128)S(1)}, u32[]{:S(2)}, u32[]{:S(2)}) async-start(f32[32,1,1024]{2,1,0:T(1,128)} %all_to_all.20), calls=%async_computation.1 | async-start | bytes 262144 | tf_op jit(solution)/shard_map/all_to_all | solution.py:79
  270.1 12.3 %all-to-all-start.2 = ((f32[32,1,1024]{2,1,0:T(1,128)}), f32[32,1,1024]{2,1,0:T(1,128)S(1)}, u32[]{:S(2)}, u32[]{:S(2)}) async-start(f32[32,1,1024]{2,1,0:T(1,128)} %copy.101), calls=%async_computation.2 | async-start | bytes 262144 | tf_op jit(solution)/shard_map/all_to_all | solution.py:95
Sparse Core Ops, SparseCore 0:
  10.2 76.2 all-gather.1
where the time goes:
time: 387 us; the launch traced here: 386 us
  matrix products  106 us (27%)
  waiting for transfers between devices  91.7 us (24%)
  blocking collectives  64.1 us (17%)
  other arithmetic  58.2 us (15%)
  local copies, waits for them, and re-layouts  27.6 us (7%)
  between operations  18.1 us (5%)
  starting transfers between devices  14.1 us (4%)
  loops' own time  6.51 us (2%)
    dot_general x9, matrix products, second_pass(): jnp.einsum('aij,aje->aie', grad_scores.astype(jnp.bfloat16), key_block, p...  74.6 us
    all_gather x1, waiting for transfers between devices, body(): everyone = lax.all_gather(teacher, 'dp', axis=0, tiled=True)  71.3 us
    psum x1, blocking collectives, body(): loss_sum = lax.psum(0.5 * (row_terms + col_terms), ('dp', 'tm'))  64.1 us
    reduce_sum x9, other arithmetic, first_pass(): col_sum = jnp.sum(jnp.exp(col_masked - col_best[:, None, :]), axis=1)  41.5 us
    dot_general x9, matrix products, first_pass(): jnp.einsum('aie,aje->aij', student, key_block, preferred_element_type=jnp...  31.2 us
    gather x1, local copies, waits for them, and re-layouts, body(): far_keys = everyone[my_dest * local_blocks + my_source]  8.78 us
  transfers between devices with their start and end apart: 4, of which 4 were waited for; matrix products, arithmetic and copies ran while one was open for 2% of the time, Pallas kernels for 0%

commit v1 on v0

--- a/solution.py
+++ b/solution.py
@@ -40,7 +40,9 @@
     own_len = lax.dynamic_slice_in_dim(valid_frames, block_base, local_blocks)
     far_len = valid_frames[(my_dest * time_count + my_tm) * local_blocks + my_source]
     query_ok = frame_ids[None, :] < own_len[:, None]
-    everyone = lax.all_gather(teacher, "dp", axis=0, tiled=True)
+    everyone = jnp.concatenate(
+        lax.all_to_all(jnp.stack([teacher] * lax.axis_size("dp")), "dp", 0, 0), axis=0
+    )
     far_keys = everyone[my_dest * local_blocks + my_source]
     keys_all = jnp.concatenate(
         [teacher[:, None], far_keys.reshape(local_blocks, partner_count, frames, proj_width)],

time: 387 us -> 518 us (1.34)
  waiting for transfers between devices: 91.7 us -> 212 us
  starting transfers between devices: 14.1 us -> 32.6 us
  between operations: 18.1 us -> 4.73 us
    all_to_all x0 -> x1, waiting for transfers between devices: none -> 199 us  [body(): lax.all_to_all(jnp.stack([teacher] * lax.axis_size('dp')), 'dp', 0, 0)]
    all_gather x1 -> x0, waiting for transfers between devices: 71.3 us -> none  [body(): everyone = lax.all_gather(teacher, 'dp', axis=0, tiled=True)]
    all_to_all x0 -> x1, starting transfers between devices: none -> 9.79 us  [body(): lax.all_to_all(jnp.stack([teacher] * lax.axis_size('dp')), 'dp', 0, 0)]
    all_to_all x1, starting transfers between devices: 5.41 us -> 15 us  [body(): lax.all_to_all(back_best, 'dp', split_axis=0, concat_axis=0, tiled=True)]
    another operation x0 -> x1, local copies, waits for them, and re-layouts: none -> 7.02 us  [body(): jnp.stack([teacher] * lax.axis_size('dp'))]
    all_to_all x1, waiting for transfers between devices: 6.85 us -> 0.01 us  [body(): lax.all_to_all(lse_out, 'dp', split_axis=0, concat_axis=0, tiled=True)]
  transfers between devices with their start and end apart: 4 -> 4, of which waited for: 4 -> 3; matrix products, arithmetic and copies ran while one was open for 2% -> 1% of each run, Pallas kernels for 0% -> 0%
where the time goes in v1:
time: 518 us; the launch traced here: 517 us
  waiting for transfers between devices  212 us (41%)
  matrix products  106 us (20%)
  blocking collectives  66.7 us (13%)
  other arithmetic  57.1 us (11%)
  starting transfers between devices  32.6 us (6%)
  local copies, waits for them, and re-layouts  31.2 us (6%)
  loops' own time  6.45 us (1%)
    all_to_all x1, waiting for transfers between devices, body(): lax.all_to_all(jnp.stack([teacher] * lax.axis_size('dp')), 'dp', 0, 0)  199 us
    dot_general x9, matrix products, second_pass(): jnp.einsum('aij,aje->aie', grad_scores.astype(jnp.bfloat16), key_block, p...  75 us
    psum x1, blocking collectives, body(): loss_sum = lax.psum(0.5 * (row_terms + col_terms), ('dp', 'tm'))  66.7 us
    reduce_sum x9, other arithmetic, first_pass(): col_sum = jnp.sum(jnp.exp(col_masked - col_best[:, None, :]), axis=1)  41.6 us
    dot_general x9, matrix products, first_pass(): jnp.einsum('aie,aje->aij', student, key_block, preferred_element_type=jnp...  31.1 us
    all_to_all x1, starting transfers between devices, body(): lax.all_to_all(back_best, 'dp', split_axis=0, concat_axis=0, tiled=True)  15 us
  transfers between devices with their start and end apart: 4, of which 3 were waited for; matrix products, arithmetic and copies ran while one was open for 1% of the time, Pallas kernels for 0%

profile of v1, /device:TPU:1, one launch (start us, length us, event | category | flops | bytes accessed | tf_op | source)
XLA Modules:
  0.0 516.5 jit_solution(17071474132606744418)
XLA Ops:
  0.6 7.0 %stack.2 = bf16[32,2,1024,128]{3,2,1,0:T(8,128)(2,1)} broadcast(bf16[2,1024,128]{2,1,0:T(8,128)(2,1)} %param.10), dimensions={1,2,3} | broadcast | bytes 17301504 | tf_op jit(solution)/shard_map/stack | solution.py:44
  7.7 9.8 %all-to-all-start = ((bf16[32,2,1024,128]{3,2,1,0:T(8,128)(2,1)}), bf16[32,2,1024,128]{3,2,1,0:T(8,128)(2,1)}, u32[]{:S(2)}, u32[]{:S(2)}) async-start(bf16[32,2,1024,128]{3,2,1,0:T(8,128)(2,1)} %stack.2), calls=%async_computation | async-start | bytes 33554432 | tf_op jit(solution)/shard_map/all_to_all | solution.py:44
  20.3 199.2 %all-to-all-done = bf16[32,2,1024,128]{3,2,1,0:T(8,128)(2,1)} async-done(((bf16[32,2,1024,128]{3,2,1,0:T(8,128)(2,1)}), bf16[32,2,1024,128]{3,2,1,0:T(8,128)(2,1)}, u32[]{:S(2)}, u32[]{:S(2)}) %all-to-all-start) | async-done | bytes 16777248 | tf_op jit(solution)/shard_map/all_to_all | solution.py:44
  219.5 8.8 %gather_fusion.1 = bf16[16,1024,128]{2,1,0:T(8,128)(2,1)} fusion(bf16[64,1024,128]{2,1,0:T(8,128)(2,1)} %bitcast.6, s32[1024]{0:T(1024)S(1)} %pad_clamp_fusion.2), kind=kCustom, calls=%fused_computation.1 | custom fusion | bytes 8388672 | tf_op jit(solution)/shard_map/gather | solution.py:46
  228.3 2.6 maximum_bitcast_fusion
  230.9 2.7 copy.96
  233.6 74.8 %while.28 = (s32[]{:T(128)}, f32[9,2,1024]{2,1,0:T(2,128)S(1)}, f32[9,2,1024]{2,1,0:T(2,128)S(1)}, f32[9,2,1024]{2,1,0:T(2,128)S(1)}, f32[9,2,1024]{2,1,0:T(2,12...) while((s32[]{:T(128)}, f32[9,2,1024]{2,1,0:T(2,128)S(1)}, ...), condition=%wide.region_5.6_spmd.clone, body=%wide.region_0.5_spmd.clone.sunk | while | flops 562032640 | bytes 17953424 | solution.py:72
  233.7 3.5 bitcast_reduce_fusion.3
  237.2 4.6 fusion.84
  242.1 3.4 bitcast_reduce_fusion.3
  245.5 4.6 fusion.84
  250.4 3.4 bitcast_reduce_fusion.3
  253.8 4.6 fusion.84
  258.7 3.5 bitcast_reduce_fusion.3
  262.1 4.6 fusion.84
  267.0 3.4 bitcast_reduce_fusion.3
  270.4 4.6 fusion.84
  275.3 3.4 bitcast_reduce_fusion.3
  278.7 4.6 fusion.84
  283.6 3.5 bitcast_reduce_fusion.3
  287.1 4.6 fusion.84
  291.9 3.4 bitcast_reduce_fusion.3
  295.4 4.6 fusion.84
  300.2 3.4 bitcast_reduce_fusion.3
  303.7 4.6 fusion.84
  308.4 0.7 scatter_custom_fusion
  309.1 0.7 all_to_all.22
  309.8 15.0 %all-to-all-start.1 = ((f32[32,1,1024]{2,1,0:T(1,128)}), f32[32,1,1024]{2,1,0:T(1,128)S(1)}, u32[]{:S(2)}, u32[]{:S(2)}) async-start(f32[32,1,1024]{2,1,0:T(1,128)} %all_to_all.22), calls=%async_computation.1 | async-start | bytes 262144 | tf_op jit(solution)/shard_map/all_to_all | solution.py:80
  326.9 0.7 all_to_all.24
  327.8 4.8 all-to-all-done.1
  332.6 3.9 all-to-all-start.2
  336.7 7.6 %all-to-all-done.2 = f32[32,1,1024]{2,1,0:T(1,128)S(1)} async-done(((f32[32,1,1024]{2,1,0:T(1,128)}), f32[32,1,1024]{2,1,0:T(1,128)S(1)}, u32[]{:S(2)}, u32[]{:S(2)}) %all-to-all-start.2) | async-done | bytes 131104 | tf_op jit(solution)/shard_map/all_to_all | solution.py:81
  344.4 0.7 select_reduce_fusion.2
  345.8 0.8 copy.101
  347.9 3.9 all-to-all-start.3
  351.8 66.7 %psum.7 = f32[]{:T(128)} all-reduce(f32[]{:T(128)S(6)} %mul.113), channel_id=1, replica_groups=mesh['dp'=32,'tm'=4] {'dp','tm'}, use_global_device_ids=true, to_apply=%region_18.19 | all-reduce | flops 1 | bytes 8 | tf_op jit(solution)/shard_map/psum | solution.py:105
  420.0 90.2 %while.29 = (s32[]{:T(128)}, f32[9,2,1024,128]{3,2,1,0:T(8,128)}, s32[9,2]{1,0:T(8,128)S(1)}, bf16[9,2,1024,128]{3,2,1,0:T(8,128)(2,1)}, bf16[2,1024,128]{2,1,0:...) while((s32[]{:T(128)}, f32[9,2,1024,128]{3,2,1,0:T(8,128)}, ...), condition=%wide.region_21.22_spmd.clone, body=%wide.region_20.21_spmd.clone.sunk | while | flops 1098911744 | bytes 4761259 | solution.py:131
  421.7 8.3 %fusion.91 = f32[9,2,1024,128]{3,2,1,0:T(8,128)} fusion(f32[9,2,1024,128]{3,2,1,0:T(8,128)} %get-tuple-element.541, s32[]{:T(128)} %get-tuple-element.540, f32[2,1024]{1,0:T(2,128)S(1)} %dynamic-slice_bitcast_fusion.3, f32[2,1024]{1,0:T(2,128)S(1)} %get-tuple-element.556, pred[1024,1024]{0,1:T(8,128)(4,1)S(1)} %fusion.89, ...), kind=kOutput, calls=%fused_computation.39.clone.1 | convolution fusion | flops 1096810496 | bytes 3692032 | tf_op jit(solution)/shard_map/while/body/eval_jaxpr/aij,aje->aie/dot_general | solution.py:123
  431.7 8.3 %fusion.91 = f32[9,2,1024,128]{3,2,1,0:T(8,128)} fusion(f32[9,2,1024,128]{3,2,1,0:T(8,128)} %get-tuple-element.541, s32[]{:T(128)} %get-tuple-element.540, f32[2,1024]{1,0:T(2,128)S(1)} %dynamic-slice_bitcast_fusion.3, f32[2,1024]{1,0:T(2,128)S(1)} %get-tuple-element.556, pred[1024,1024]{0,1:T(8,128)(4,1)S(1)} %fusion.89, ...), kind=kOutput, calls=%fused_computation.39.clone.1 | convolution fusion | flops 1096810496 | bytes 3692032 | tf_op jit(solution)/shard_map/while/body/eval_jaxpr/aij,aje->aie/dot_general | solution.py:123
  441.7 8.3 %fusion.91 = f32[9,2,1024,128]{3,2,1,0:T(8,128)} fusion(f32[9,2,1024,128]{3,2,1,0:T(8,128)} %get-tuple-element.541, s32[]{:T(128)} %get-tuple-element.540, f32[2,1024]{1,0:T(2,128)S(1)} %dynamic-slice_bitcast_fusion.3, f32[2,1024]{1,0:T(2,128)S(1)} %get-tuple-element.556, pred[1024,1024]{0,1:T(8,128)(4,1)S(1)} %fusion.89, ...), kind=kOutput, calls=%fused_computation.39.clone.1 | convolution fusion | flops 1096810496 | bytes 3692032 | tf_op jit(solution)/shard_map/while/body/eval_jaxpr/aij,aje->aie/dot_general | solution.py:123
  451.7 8.3 %fusion.91 = f32[9,2,1024,128]{3,2,1,0:T(8,128)} fusion(f32[9,2,1024,128]{3,2,1,0:T(8,128)} %get-tuple-element.541, s32[]{:T(128)} %get-tuple-element.540, f32[2,1024]{1,0:T(2,128)S(1)} %dynamic-slice_bitcast_fusion.3, f32[2,1024]{1,0:T(2,128)S(1)} %get-tuple-element.556, pred[1024,1024]{0,1:T(8,128)(4,1)S(1)} %fusion.89, ...), kind=kOutput, calls=%fused_computation.39.clone.1 | convolution fusion | flops 1096810496 | bytes 3692032 | tf_op jit(solution)/shard_map/while/body/eval_jaxpr/aij,aje->aie/dot_general | solution.py:123
  461.7 8.3 %fusion.91 = f32[9,2,1024,128]{3,2,1,0:T(8,128)} fusion(f32[9,2,1024,128]{3,2,1,0:T(8,128)} %get-tuple-element.541, s32[]{:T(128)} %get-tuple-element.540, f32[2,1024]{1,0:T(2,128)S(1)} %dynamic-slice_bitcast_fusion.3, f32[2,1024]{1,0:T(2,128)S(1)} %get-tuple-element.556, pred[1024,1024]{0,1:T(8,128)(4,1)S(1)} %fusion.89, ...), kind=kOutput, calls=%fused_computation.39.clone.1 | convolution fusion | flops 1096810496 | bytes 3692032 | tf_op jit(solution)/shard_map/while/body/eval_jaxpr/aij,aje->aie/dot_general | solution.py:123
  471.7 8.3 %fusion.91 = f32[9,2,1024,128]{3,2,1,0:T(8,128)} fusion(f32[9,2,1024,128]{3,2,1,0:T(8,128)} %get-tuple-element.541, s32[]{:T(128)} %get-tuple-element.540, f32[2,1024]{1,0:T(2,128)S(1)} %dynamic-slice_bitcast_fusion.3, f32[2,1024]{1,0:T(2,128)S(1)} %get-tuple-element.556, pred[1024,1024]{0,1:T(8,128)(4,1)S(1)} %fusion.89, ...), kind=kOutput, calls=%fused_computation.39.clone.1 | convolution fusion | flops 1096810496 | bytes 3692032 | tf_op jit(solution)/shard_map/while/body/eval_jaxpr/aij,aje->aie/dot_general | solution.py:123
  481.7 8.3 %fusion.91 = f32[9,2,1024,128]{3,2,1,0:T(8,128)} fusion(f32[9,2,1024,128]{3,2,1,0:T(8,128)} %get-tuple-element.541, s32[]{:T(128)} %get-tuple-element.540, f32[2,1024]{1,0:T(2,128)S(1)} %dynamic-slice_bitcast_fusion.3, f32[2,1024]{1,0:T(2,128)S(1)} %get-tuple-element.556, pred[1024,1024]{0,1:T(8,128)(4,1)S(1)} %fusion.89, ...), kind=kOutput, calls=%fused_computation.39.clone.1 | convolution fusion | flops 1096810496 | bytes 3692032 | tf_op jit(solution)/shard_map/while/body/eval_jaxpr/aij,aje->aie/dot_general | solution.py:123
  491.8 8.4 %fusion.91 = f32[9,2,1024,128]{3,2,1,0:T(8,128)} fusion(f32[9,2,1024,128]{3,2,1,0:T(8,128)} %get-tuple-element.541, s32[]{:T(128)} %get-tuple-element.540, f32[2,1024]{1,0:T(2,128)S(1)} %dynamic-slice_bitcast_fusion.3, f32[2,1024]{1,0:T(2,128)S(1)} %get-tuple-element.556, pred[1024,1024]{0,1:T(8,128)(4,1)S(1)} %fusion.89, ...), kind=kOutput, calls=%fused_computation.39.clone.1 | convolution fusion | flops 1096810496 | bytes 3692032 | tf_op jit(solution)/shard_map/while/body/eval_jaxpr/aij,aje->aie/dot_general | solution.py:123
  501.8 8.4 %fusion.91 = f32[9,2,1024,128]{3,2,1,0:T(8,128)} fusion(f32[9,2,1024,128]{3,2,1,0:T(8,128)} %get-tuple-element.541, s32[]{:T(128)} %get-tuple-element.540, f32[2,1024]{1,0:T(2,128)S(1)} %dynamic-slice_bitcast_fusion.3, f32[2,1024]{1,0:T(2,128)S(1)} %get-tuple-element.556, pred[1024,1024]{0,1:T(8,128)(4,1)S(1)} %fusion.89, ...), kind=kOutput, calls=%fused_computation.39.clone.1 | convolution fusion | flops 1096810496 | bytes 3692032 | tf_op jit(solution)/shard_map/while/body/eval_jaxpr/aij,aje->aie/dot_general | solution.py:123
  510.2 4.3 reduce_sum.113
  514.5 0.9 multiply_convert_fusion
  (154 shorter events, 16.8 us)
Async XLA Ops:
  7.6 9.9 %copy-start.3 = (s32[256,8]{0,1:T(8,128)S(1)}, s32[256,8]{0,1:T(8,128)}, u32[]{:S(2)}) copy-start(s32[256,8]{0,1:T(8,128)} %param.12) | copy-start | bytes 24580
  7.7 10.1 %copy-start.4 = (s32[256,8]{0,1:T(8,128)S(1)}, s32[256,8]{0,1:T(8,128)}, u32[]{:S(2)}) copy-start(s32[256,8]{0,1:T(8,128)} %param.11) | copy-start | bytes 24580
  7.7 10.9 %copy-start = (s32[256]{0:T(256)S(1)}, s32[256]{0:T(256)}, u32[]{:S(2)}) copy-start(s32[256]{0:T(256)} %param.13) | copy-start | bytes 3076
  7.7 12.2 %copy-start.1 = (bf16[2,1024,128]{2,1,0:T(8,128)(2,1)S(1)}, bf16[2,1024,128]{2,1,0:T(8,128)(2,1)}, u32[]{:S(2)}) copy-start(bf16[2,1024,128]{2,1,0:T(8,128)(2,1)} %param.10) | copy-start | bytes 1572868
  7.7 12.2 %copy-start.2 = (bf16[2,1024,128]{2,1,0:T(8,128)(2,1)S(1)}, bf16[2,1024,128]{2,1,0:T(8,128)(2,1)}, u32[]{:S(2)}) copy-start(bf16[2,1024,128]{2,1,0:T(8,128)(2,1)} %param.9) | copy-start | bytes 1572868
  7.7 211.9 %all-to-all-start = ((bf16[32,2,1024,128]{3,2,1,0:T(8,128)(2,1)}), bf16[32,2,1024,128]{3,2,1,0:T(8,128)(2,1)}, u32[]{:S(2)}, u32[]{:S(2)}) async-start(bf16[32,2,1024,128]{3,2,1,0:T(8,128)(2,1)} %stack.2), calls=%async_computation | async-start | bytes 33554432 | tf_op jit(solution)/shard_map/all_to_all | solution.py:44
  309.8 22.7 %all-to-all-start.1 = ((f32[32,1,1024]{2,1,0:T(1,128)}), f32[32,1,1024]{2,1,0:T(1,128)S(1)}, u32[]{:S(2)}, u32[]{:S(2)}) async-start(f32[32,1,1024]{2,1,0:T(1,128)} %all_to_all.22), calls=%async_computation.1 | async-start | bytes 262144 | tf_op jit(solution)/shard_map/all_to_all | solution.py:80
  332.6 11.6 %all-to-all-start.2 = ((f32[32,1,1024]{2,1,0:T(1,128)}), f32[32,1,1024]{2,1,0:T(1,128)S(1)}, u32[]{:S(2)}, u32[]{:S(2)}) async-start(f32[32,1,1024]{2,1,0:T(1,128)} %all_to_all.24), calls=%async_computation.2 | async-start | bytes 262144 | tf_op jit(solution)/shard_map/all_to_all | solution.py:81
  347.9 71.4 %all-to-all-start.3 = ((f32[32,1,1024]{2,1,0:T(1,128)}), f32[32,1,1024]{2,1,0:T(1,128)S(1)}, u32[]{:S(2)}, u32[]{:S(2)}) async-start(f32[32,1,1024]{2,1,0:T(1,128)} %copy.101), calls=%async_computation.3 | async-start | bytes 262144 | tf_op jit(solution)/shard_map/all_to_all | solution.py:97
